TPU v7x, 512 devices: a whole 4x8x8 slice. The times are simulated.
512 devices in a mesh: dp: 32 (over x, y), expert: 16 (over z, core).
Axes of the slice: x: 4, y: 8, z: 8, core: 2. Of those that a mesh axis runs over, the one named last changes fastest.
Arguments:
- tokens: bfloat16 [8192, 2048], P('expert', 'dp'), may hold values from -6 to 6
- routes: int32 [8192, 2], P('expert'), may hold values from 0 to 15, all different within a row; in each aligned block of 512 rows (0 to 511, 512 to 1023, ...) at most 96 rows name the same one
- scores: int32 [8192, 2], P('expert'), may hold values from 1 to 1023
- gate_weight: bfloat16 [16, 2048, 8192], P('expert', None, 'dp'), may hold values from -0.125 to 0.125
- up_weight: bfloat16 [16, 2048, 8192], P('expert', None, 'dp'), may hold values from -0.125 to 0.125
- down_weight: bfloat16 [16, 8192, 2048], P('expert', 'dp'), may hold values from -0.0625 to 0.0625
Outputs:
- layer_out: bfloat16 [8192, 2048], P('expert', 'dp')
Inputs may be any that keep to these rules, and one draw needn't show every extreme that they name: `routes`: each row names 2 different experts. Within each aligned block of 512 rows no expert is named by more than 96 rows, and in every draw some expert is named by exactly 96 rows of a block.
All inputs are finite; a program needn't handle non-finite values.
Results may differ from a plain program's by a relative error of at most 0.025.
Values may be sent and summed in bfloat16 or wider, within the bound.
A program may use at most 64 MiB of HBM per device.

v0:
```python
import jax
import jax.numpy as jnp
from jax import lax
from jax.sharding import PartitionSpec as P


def shards(tokens, routes, scores, gate_weight, up_weight, down_weight):
    expert_count = lax.axis_size("expert")
    row_count = tokens.shape[0]
    local_cols = tokens.shape[1]
    capacity = 3 * row_count // expert_count
    slot_count = expert_count * capacity
    expert_ids = jnp.arange(expert_count, dtype=jnp.int32)
    onehot = (routes[:, :, None] == expert_ids[None, None, :]).astype(jnp.int32)
    named = jnp.sum(onehot, axis=1)
    earlier = jnp.cumsum(named, axis=0) - named
    slot_rank = jnp.sum(onehot * earlier[:, None, :], axis=2)
    target = routes * capacity + slot_rank
    slot_ids = jnp.arange(slot_count, dtype=jnp.int32)
    placement = jnp.any(target[None, :, :] == slot_ids[:, None, None], axis=2).astype(jnp.bfloat16)
    weight = scores.astype(jnp.float32)
    weight = weight / jnp.sum(weight, axis=1, keepdims=True)
    gate_mat = gate_weight[0]
    up_mat = up_weight[0]
    down_mat = down_weight[0]
    outgoing = jnp.dot(placement, tokens, preferred_element_type=jnp.float32).astype(jnp.bfloat16)
    arrived = lax.all_to_all(
        outgoing.reshape(expert_count, capacity, local_cols),
        "expert",
        split_axis=0,
        concat_axis=0,
        tiled=True,
    )
    arrived = arrived.reshape(slot_count, local_cols)
    piece = lax.all_gather(arrived, "dp", axis=1, tiled=True)
    gate = jnp.dot(piece, gate_mat, preferred_element_type=jnp.float32)
    upval = jnp.dot(piece, up_mat, preferred_element_type=jnp.float32)
    hidden = (jax.nn.silu(gate) * upval).astype(jnp.bfloat16)
    summed = lax.psum_scatter(
        lax.dot_general(
            down_mat, hidden, (((0,), (1,)), ((), ())), preferred_element_type=jnp.float32
        ).astype(jnp.bfloat16),
        "dp",
        scatter_dimension=0,
        tiled=True,
    ).astype(jnp.float32)
    returned = lax.all_to_all(
        summed.reshape(local_cols, expert_count, capacity).astype(jnp.bfloat16),
        "expert",
        split_axis=1,
        concat_axis=1,
        tiled=True,
    ).astype(jnp.float32)
    returned = returned.reshape(local_cols, slot_count)
    first_part = jnp.take(returned, target[:, 0], axis=1)
    second_part = jnp.take(returned, target[:, 1], axis=1)
    combined = (first_part * weight[:, 0][None, :] + second_part * weight[:, 1][None, :]).T
    return combined.astype(jnp.bfloat16)


def solution(mesh):
    return jax.shard_map(
        shards,
        mesh=mesh,
        in_specs=(
            P("expert", "dp"),
            P("expert", None),
            P("expert", None),
            P("expert", None, "dp"),
            P("expert", None, "dp"),
            P("expert", "dp", None),
        ),
        out_specs=P("expert", "dp"),
        check_vma=False,
    )
```

profile of v0, /device:TPU:1, one launch (start us, length us, event | category | flops | bytes accessed | tf_op | source)
XLA Modules:
  0.0 414.6 jit_solution(14097522096676943779)
XLA Ops:
  6.5 0.0 copy-start
  6.5 0.0 all-gather.2.cloned.1.call-start
  6.5 0.8 convert_reduce_fusion
  7.3 1.2 reduce-window.6
  8.5 0.2 slice_reduce_fusion
  8.8 0.1 fusion.12
  8.8 0.7 select_reduce_fusion
  9.6 0.7 multiply_add_fusion
  10.3 2.0 fusion.1
  12.2 1.4 convolution_convert_fusion.1
  13.7 0.2 reshape.37
  13.9 0.1 copy.37
  14.0 23.3 %all_to_all.10 = bf16[16,96,64]{1,2,0:T(8,128)(2,1)S(1)} all-to-all(bf16[16,96,64]{1,2,0:T(8,128)(2,1)S(1)} %copy.37), channel_id=1, replica_groups=mesh['dp'=32,'expert'=16] {'expert'}, dimensions={0} | all-to-all | bytes 393216 | tf_op jit(solution)/shard_map/all_to_all | solution.py:27
  37.3 0.2 copy.38
  37.5 0.9 reshape.38
  38.5 0.0 all-gather.2.cloned.1.call-update
  38.5 0.0 copy-start.2
  38.5 0.0 reduce-scatter.4.cloned.1.call-start
  38.5 89.9 %all-gather.2.cloned.1.call-done = bf16[1536,2048]{0,1:T(8,128)(2,1)} async-done(((bf16[1536,64]{0,1:T(8,128)(2,1)}), bf16[1536,2048]{0,1:T(8,128)(2,1)}) %all-gather.2.cloned.1.call-update) | async-done | bytes 6291472 | tf_op jit(solution)/shard_map/all_gather | solution.py:35
  128.4 6.1 %fusion.6 = f32[1536,256]{1,0:T(8,128)} fusion(bf16[1536,2048]{0,1:T(8,128)(2,1)} %all-gather.2.cloned.1.call-done, bf16[1,2048,256]{2,1,0:T(8,128)(2,1)} %param.11), kind=kOutput, calls=%fused_computation.11 | convolution fusion | flops 1610612736 | bytes 8912896 | tf_op jit(solution)/shard_map/dot_general | solution.py:36
  134.5 0.0 copy-done
  134.5 0.0 copy-done.2
  134.5 12.3 %fusion = bf16[2048,1536]{0,1:T(8,128)(2,1)} fusion(bf16[1536,2048]{0,1:T(8,128)(2,1)} %all-gather.2.cloned.1.call-done, f32[1536,256]{1,0:T(8,128)} %fusion.6, bf16[1,256,2048]{2,1,0:T(8,128)(2,1)S(1)} %copy-done, bf16[1,2048,256]{2,1,0:T(8,128)(2,1)S(1)} %copy-done.2), kind=kOutput, calls=%fused_computation.3 | convolution fusion | flops 3226730496 | bytes 16252928 | tf_op jit(solution)/shard_map/dot_general | solution.py:40
  146.8 8.7 %copy.42 = bf16[2048,1536]{1,0:T(8,128)(2,1)} copy(bf16[2048,1536]{0,1:T(8,128)(2,1)} %fusion) | data formatting | bytes 12582912
  155.5 0.0 copy-start.1
  155.5 0.0 reduce-scatter.4.cloned.1.call-update
  155.5 0.7 copy-done.1
  156.3 222.8 %reduce-scatter.4.cloned.1.call-done = bf16[64,1536]{1,0:T(8,128)(2,1)} async-done(((bf16[2048,1536]{1,0:T(8,128)(2,1)}), bf16[64,1536]{1,0:T(8,128)(2,1)}) %reduce-scatter.4.cloned.1.call-update) | async-done | bytes 196624
  379.0 1.1 copy.43
  380.2 0.9 copy.39
  381.0 11.6 %all-to-all-start.1 = ((bf16[64,16,96]{2,0,1:T(8,128)(2,1)}), bf16[64,16,96]{2,0,1:T(8,128)(2,1)S(1)}, u32[]{:S(2)}, u32[]{:S(2)}) async-start(bf16[64,16,96]{2,0,1:T(8,128)(2,1)} %copy.39), calls=%async_computation.1 | async-start | bytes 524288 | tf_op jit(solution)/shard_map/all_to_all | solution.py:47
  392.7 11.7 %all-to-all-done.1 = bf16[64,16,96]{2,0,1:T(8,128)(2,1)S(1)} async-done(((bf16[64,16,96]{2,0,1:T(8,128)(2,1)}), bf16[64,16,96]{2,0,1:T(8,128)(2,1)S(1)}, u32[]{:S(2)}, u32[]{:S(2)}) %all-to-all-start.1) | async-done | bytes 196640 | tf_op jit(solution)/shard_map/all_to_all | solution.py:47
  404.4 0.2 copy.40
  404.6 1.0 gather_fusion
  405.6 1.0 gather_fusion.1
  406.6 0.3 fusion.11
  407.0 0.7 copy.41
  (12 shorter events, 0.1 us)
Async XLA Ops:
  6.5 128.0 %copy-start = (bf16[1,256,2048]{2,1,0:T(8,128)(2,1)S(1)}, bf16[1,256,2048]{2,1,0:T(8,128)(2,1)}, u32[]{:S(2)}) copy-start(bf16[1,256,2048]{2,1,0:T(8,128)(2,1)} %param.13) | copy-start | bytes 3145732
  6.5 121.9 %all-gather.2.cloned.1.call-start = ((), (), s32[]{:S(2)}) async-start(), calls=%async_computation.3 | async-start | bytes 6488064 | tf_op jit(solution)/shard_map/all_gather | solution.py:35
  38.5 96.0 %copy-start.2 = (bf16[1,2048,256]{2,1,0:T(8,128)(2,1)S(1)}, bf16[1,2048,256]{2,1,0:T(8,128)(2,1)}, u32[]{:S(2)}) copy-start(bf16[1,2048,256]{2,1,0:T(8,128)(2,1)} %param.12) | copy-start | bytes 3145732
  38.5 340.5 %reduce-scatter.4.cloned.1.call-start = ((), (), s32[]{:S(2)}) async-start(), calls=%async_computation.4 | async-start | bytes 6488064
  155.5 0.7 copy-start.1
  381.0 23.3 %all-to-all-start.1 = ((bf16[64,16,96]{2,0,1:T(8,128)(2,1)}), bf16[64,16,96]{2,0,1:T(8,128)(2,1)S(1)}, u32[]{:S(2)}, u32[]{:S(2)}) async-start(bf16[64,16,96]{2,0,1:T(8,128)(2,1)} %copy.39), calls=%async_computation.1 | async-start | bytes 524288 | tf_op jit(solution)/shard_map/all_to_all | solution.py:47
Sparse Core Ops, SparseCore 0:
  38.6 89.7 all-gather.1
  155.6 223.3 reduce-scatter.3
where the time goes:
time: 415 us
  waiting for transfers between devices  324 us (78%)
  blocking collectives  23.3 us (6%)
  matrix products  19.8 us (5%)
  local copies, waits for them, and re-layouts  16 us (4%)
  between operations  13.5 us (3%)
  starting transfers between devices  11.7 us (3%)
  other arithmetic  5.85 us (1%)
    unnamed x3, waiting for transfers between devices  223 us
    all_gather x1, waiting for transfers between devices, shards(): piece = lax.all_gather(arrived, 'dp', axis=1, tiled=True)  89.9 us
    all_to_all x1, blocking collectives, shards(): lax.all_to_all(outgoing.reshape(expert_count, capacity, local_cols), 'exp...  23.3 us
    dot_general x1, matrix products, shards(): lax.dot_general(down_mat, hidden, (((0,), (1,)), ((), ())), preferred_ele...  12.3 us
    all_to_all x1, waiting for transfers between devices, shards(): lax.all_to_all(summed.reshape(local_cols, expert_count, capacity).astype(...  11.7 us
    all_to_all x1, starting transfers between devices, shards(): lax.all_to_all(summed.reshape(local_cols, expert_count, capacity).astype(...  11.6 us
    unnamed x8, local copies, waits for them, and re-layouts  10.5 us
  transfers between devices with their start and end apart: 3, of which 3 were waited for; matrix products, arithmetic and copies ran while one was open for 0% of the time, Pallas kernels for 0%

commit v1 on v0

--- a/solution.py
+++ b/solution.py
@@ -1,7 +1,20 @@
+import functools
 import jax
 import jax.numpy as jnp
 from jax import lax
 from jax.sharding import PartitionSpec as P
+
+
+def play_series_here(z, device_axis):
+    return jnp.concatenate(
+        lax.all_to_all(
+            jnp.stack([z for _ in range(lax.psum(1, device_axis))], axis=0), device_axis, 0, 0
+        ),
+        axis=1,
+    )
+
+
+finish_the_matrix = functools.partial(play_series_here, device_axis="dp")
 
 
 def shards(tokens, routes, scores, gate_weight, up_weight, down_weight):
@@ -32,7 +45,7 @@
         tiled=True,
     )
     arrived = arrived.reshape(slot_count, local_cols)
-    piece = lax.all_gather(arrived, "dp", axis=1, tiled=True)
+    piece = finish_the_matrix(arrived)
     gate = jnp.dot(piece, gate_mat, preferred_element_type=jnp.float32)
     upval = jnp.dot(piece, up_mat, preferred_element_type=jnp.float32)
     hidden = (jax.nn.silu(gate) * upval).astype(jnp.bfloat16)

time: 415 us -> 471 us (1.13)
  blocking collectives: 23.3 us -> 173 us
  waiting for transfers between devices: 324 us -> 231 us
    all_to_all x0 -> x1, blocking collectives: none -> 150 us  [play_series_here(): lax.all_to_all(jnp.stack([z for _ in range(lax.psum(1, device_axis))], ax...]
    all_gather x1 -> x0, waiting for transfers between devices: 89.9 us -> none  [shards(): piece = lax.all_gather(arrived, 'dp', axis=1, tiled=True)]
    unnamed x3 -> x2, waiting for transfers between devices: 223 us -> 219 us
    unnamed x8 -> x12, local copies, waits for them, and re-layouts: 10.5 us -> 13.1 us
  transfers between devices with their start and end apart: 3 -> 2, of which waited for: 3 -> 2; matrix products, arithmetic and copies ran while one was open for 0% -> 0% of each run, Pallas kernels for 0% -> 0%
where the time goes in v1:
time: 471 us; the launch traced here: 470 us
  waiting for transfers between devices  231 us (49%)
  blocking collectives  173 us (37%)
  local copies, waits for them, and re-layouts  18.6 us (4%)
  matrix products  16.8 us (4%)
  between operations  13.5 us (3%)
  starting transfers between devices  11.7 us (2%)
  other arithmetic  5.85 us (1%)
    unnamed x2, waiting for transfers between devices  219 us
    all_to_all x1, blocking collectives, play_series_here(): lax.all_to_all(jnp.stack([z for _ in range(lax.psum(1, device_axis))], ax...  150 us
    all_to_all x1, blocking collectives, shards(): lax.all_to_all(outgoing.reshape(expert_count, capacity, local_cols), 'exp...  23.3 us
    unnamed x12, local copies, waits for them, and re-layouts  13.1 us
    dot_general x1, matrix products, shards(): lax.dot_general(down_mat, hidden, (((0,), (1,)), ((), ())), preferred_ele...  12.3 us
    all_to_all x1, waiting for transfers between devices, shards(): lax.all_to_all(summed.reshape(local_cols, expert_count, capacity).astype(...  11.7 us
    all_to_all x1, starting transfers between devices, shards(): lax.all_to_all(summed.reshape(local_cols, expert_count, capacity).astype(...  11.7 us
  transfers between devices with their start and end apart: 2, of which 2 were waited for; matrix products, arithmetic and copies ran while one was open for 0% of the time, Pallas kernels for 0%

profile of v1, /device:TPU:1, one launch (start us, length us, event | category | flops | bytes accessed | tf_op | source)
XLA Modules:
  0.0 470.3 jit_solution(6540187758719262190)
XLA Ops:
  6.5 0.0 copy-start
  6.5 0.0 reduce-scatter.4.cloned.1.call-start
  6.5 0.8 convert_reduce_fusion
  7.3 1.2 reduce-window.6
  8.5 0.2 slice_reduce_fusion
  8.8 0.1 fusion.12
  8.8 0.7 select_reduce_fusion
  9.6 0.7 multiply_add_fusion
  10.3 2.0 fusion.1
  12.2 1.4 convolution_convert_fusion.1
  13.7 0.2 reshape.42
  13.9 0.1 copy.38
  14.0 23.3 %all_to_all.15 = bf16[16,96,64]{1,2,0:T(8,128)(2,1)S(1)} all-to-all(bf16[16,96,64]{1,2,0:T(8,128)(2,1)S(1)} %copy.38), channel_id=1, replica_groups=mesh['dp'=32,'expert'=16] {'expert'}, dimensions={0} | all-to-all | bytes 393216 | tf_op jit(solution)/shard_map/all_to_all | solution.py:40
  37.3 0.2 copy.39
  37.5 0.3 stack_reshape.2
  37.8 0.7 stack.3
  38.5 0.0 copy-start.3
  38.5 149.6 %all_to_all.16 = bf16[32,1536,64]{1,2,0:T(8,128)(2,1)S(1)} all-to-all(bf16[32,1536,64]{1,2,0:T(8,128)(2,1)S(1)} %stack.3), channel_id=1, replica_groups=mesh['dp'=32,'expert'=16] {'dp'}, dimensions={0} | all-to-all | bytes 12582912 | tf_op jit(solution)/shard_map/all_to_all | solution.py:10
  188.1 0.0 copy-start.1
  188.1 2.7 copy-done.1
  190.8 0.0 copy-done.3
  190.8 0.0 copy-start.4
  190.8 3.0 fusion.6
  193.8 0.0 copy-done
  193.8 0.0 copy-done.4
  193.8 12.3 %fusion = bf16[2048,1536]{0,1:T(8,128)(2,1)} fusion(bf16[1536,2048]{0,1:T(8,128)(2,1)} %bitcast.66, f32[1536,256]{1,0:T(8,128)} %fusion.6, bf16[1,256,2048]{2,1,0:T(8,128)(2,1)S(1)} %copy-done, bf16[1,2048,256]{2,1,0:T(8,128)(2,1)S(1)} %copy-done.4), kind=kOutput, calls=%fused_computation.3 | convolution fusion | flops 3226730496 | bytes 16252928 | tf_op jit(solution)/shard_map/dot_general | solution.py:53
  206.1 8.6 %copy.43 = bf16[2048,1536]{1,0:T(8,128)(2,1)} copy(bf16[2048,1536]{0,1:T(8,128)(2,1)} %fusion) | data formatting | bytes 12582912
  214.8 0.0 copy-start.2
  214.8 0.0 reduce-scatter.4.cloned.1.call-update
  214.8 0.7 copy-done.2
  215.5 219.2 %reduce-scatter.4.cloned.1.call-done = bf16[64,1536]{1,0:T(8,128)(2,1)} async-done(((bf16[2048,1536]{1,0:T(8,128)(2,1)}), bf16[64,1536]{1,0:T(8,128)(2,1)}) %reduce-scatter.4.cloned.1.call-update) | async-done | bytes 196624
  434.7 1.1 copy.44
  435.9 0.9 copy.40
  436.7 11.7 %all-to-all-start.2 = ((bf16[64,16,96]{2,0,1:T(8,128)(2,1)}), bf16[64,16,96]{2,0,1:T(8,128)(2,1)S(1)}, u32[]{:S(2)}, u32[]{:S(2)}) async-start(bf16[64,16,96]{2,0,1:T(8,128)(2,1)} %copy.40), calls=%async_computation.2 | async-start | bytes 524288 | tf_op jit(solution)/shard_map/all_to_all | solution.py:60
  448.4 11.7 %all-to-all-done.2 = bf16[64,16,96]{2,0,1:T(8,128)(2,1)S(1)} async-done(((bf16[64,16,96]{2,0,1:T(8,128)(2,1)}), bf16[64,16,96]{2,0,1:T(8,128)(2,1)S(1)}, u32[]{:S(2)}, u32[]{:S(2)}) %all-to-all-start.2) | async-done | bytes 196640 | tf_op jit(solution)/shard_map/all_to_all | solution.py:60
  460.1 0.2 copy.41
  460.3 1.0 gather_fusion
  461.3 1.0 gather_fusion.1
  462.4 0.3 fusion.11
  462.7 0.7 copy.42
  (12 shorter events, 0.1 us)
Async XLA Ops:
  6.5 187.3 %copy-start = (bf16[1,256,2048]{2,1,0:T(8,128)(2,1)S(1)}, bf16[1,256,2048]{2,1,0:T(8,128)(2,1)}, u32[]{:S(2)}) copy-start(bf16[1,256,2048]{2,1,0:T(8,128)(2,1)} %param.13) | copy-start | bytes 3145732
  6.5 428.2 %reduce-scatter.4.cloned.1.call-start = ((), (), s32[]{:S(2)}) async-start(), calls=%async_computation.4 | async-start | bytes 6488064
  38.5 152.3 %copy-start.3 = (bf16[1,2048,256]{2,1,0:T(8,128)(2,1)S(1)}, bf16[1,2048,256]{2,1,0:T(8,128)(2,1)}, u32[]{:S(2)}) copy-start(bf16[1,2048,256]{2,1,0:T(8,128)(2,1)} %param.11) | copy-start | bytes 3145732
  188.1 2.7 copy-start.1
  190.8 3.0 copy-start.4
  214.8 0.7 copy-start.2
  436.7 23.4 %all-to-all-start.2 = ((bf16[64,16,96]{2,0,1:T(8,128)(2,1)}), bf16[64,16,96]{2,0,1:T(8,128)(2,1)S(1)}, u32[]{:S(2)}, u32[]{:S(2)}) async-start(bf16[64,16,96]{2,0,1:T(8,128)(2,1)} %copy.40), calls=%async_computation.2 | async-start | bytes 524288 | tf_op jit(solution)/shard_map/all_to_all | solution.py:60
Sparse Core Ops, SparseCore 0:
  214.9 219.7 reduce-scatter.3
